TPU v7x, 128 devices: a whole 4x4x4 slice. The times are simulated.
128 devices in a mesh: dp: 16 (over x_lo, y, core), tensor: 8 (over x_hi, z).
Axes of the slice: x: 4 (x_hi: 2, x_lo: 2; x = x_hi * 2 + x_lo), y: 4, z: 4, core: 2. Of those that a mesh axis runs over, the one named last changes fastest.
Arguments:
- block_input: bfloat16 [32768, 768], P(('dp', 'tensor')), may hold values from -6 to 6
- w_value: bfloat16 [768, 768], replicated, may hold values from -0.21875 to 0.21875
- b_value: bfloat16 [768], replicated, may hold values from -2 to 2
- conv_kernel: bfloat16 [65, 768], replicated, may hold values from -0.75 to 0.75
- w_out: bfloat16 [768, 768], replicated, may hold values from -0.21875 to 0.21875
- b_out: bfloat16 [768], replicated, may hold values from -2 to 2
- gain_attn: bfloat16 [768], replicated, may hold values from 0.5 to 1.5
- shift_attn: bfloat16 [768], replicated, may hold values from -2 to 2
- w_up: bfloat16 [768, 3072], P(None, 'tensor'), may hold values from -0.21875 to 0.21875
- b_up: bfloat16 [3072], P('tensor'), may hold values from -2 to 2
- w_down: bfloat16 [3072, 768], P('tensor'), may hold values from -0.109375 to 0.109375
- b_down: bfloat16 [768], replicated, may hold values from -2 to 2
- gain_ffn: bfloat16 [768], replicated, may hold values from 0.5 to 1.5
- shift_ffn: bfloat16 [768], replicated, may hold values from -2 to 2
- query_codes: int32 [32768, 384], P(('dp', 'tensor')), may hold values from 0 to 255
- key_codes: int32 [32768, 384], P(('dp', 'tensor')), may hold values from 0 to 255
- key_live: int32 [32768], P(('dp', 'tensor')), may hold values 0 or 1
- seq_lengths: int32 [128, 4], P(('dp', 'tensor')), may hold values from 1 to 128, 256 in all within a row
- out_grad: bfloat16 [32768, 768], P(('dp', 'tensor')), may hold values from -6 to 6
Outputs:
- block_output: bfloat16 [32768, 768], P(('dp', 'tensor'))
- input_grad: float32 [32768, 768], P(('dp', 'tensor'))
- grad_w_value: float32 [768, 768], replicated
- grad_b_value: float32 [768], replicated
- grad_conv_kernel: float32 [65, 768], replicated
- grad_w_out: float32 [768, 768], replicated
- grad_b_out: float32 [768], replicated
- grad_gain_attn: float32 [768], replicated
- grad_shift_attn: float32 [768], replicated
- grad_w_up: float32 [768, 3072], P(None, 'tensor')
- grad_b_up: float32 [3072], P('tensor')
- grad_w_down: float32 [3072, 768], P('tensor')
- grad_b_down: float32 [768], replicated
- grad_gain_ffn: float32 [768], replicated
- grad_shift_ffn: float32 [768], replicated
Inputs may be any that keep to these rules, and one draw needn't show every extreme that they name: `seq_lengths`: each item's lengths sum to 256; the longest is 128. `key_live`: 1 marks a live key, 0 a padded one. `query_codes`: column h * 32 + s holds head h's code in hash set s. `key_codes`: column h * 32 + s holds head h's code in hash set s.
All inputs are finite; a program needn't handle non-finite values. No bound on the sum of `key_live` on one device may be relied on, other than what follows from the above.
Results may differ from a plain program's by a relative error of at most 0.02.
Values may be sent and summed in bfloat16 or wider, within the bound.
No kernel may reach another device: no remote copies, remote signals or barrier semaphores. Data moves between devices by JAX's collectives and lax.ppermute only.
A program may use at most 128 MiB of HBM per device.

v0:
```python
from functools import partial
import jax
import jax.numpy as jnp
from jax import lax
from jax.sharding import PartitionSpec as P

HEADS = 12
SETS = 32
BUCKETS = 256


def dot_last(former, latter):
    return lax.dot_general(
        former, latter, (((1,), (1,)), ((), ())), preferred_element_type=jnp.float32
    )


def dot_first(former, latter):
    return lax.dot_general(
        former, latter, (((0,), (0,)), ((), ())), preferred_element_type=jnp.float32
    )


def layer_norm(residual, gain_vec, shift_vec):
    average = jnp.mean(residual, axis=-1, keepdims=True)
    centred = residual - average
    variance = jnp.mean(centred * centred, axis=-1, keepdims=True)
    return centred * lax.rsqrt(variance + 1e-05) * gain_vec + shift_vec


def head_norm(mixed, head_count, head_dim):
    grouped = mixed.reshape(mixed.shape[0], head_count, head_dim)
    scaling = lax.rsqrt(jnp.mean(grouped * grouped, axis=-1, keepdims=True) + 1e-06)
    return (grouped * scaling).reshape(mixed.shape)


def gelu_exact(pre_act):
    return jax.nn.gelu(pre_act, approximate=False)


def depth_conv(values, kernel, segment):
    taps = kernel.shape[0]
    margin = taps // 2
    length = values.shape[0]
    padded = jnp.pad(values, ((margin, margin), (0, 0)))
    seg_padded = jnp.pad(segment, (margin, margin), constant_values=-1)
    running = jnp.zeros_like(values)
    for offset in range(taps):
        joined = (seg_padded[offset : offset + length] == segment).astype(jnp.float32)[:, None]
        running = running + padded[offset : offset + length] * joined * kernel[offset][None, :]
    return running


def conv_back(grad_out, values, kernel, segment):
    taps = kernel.shape[0]
    margin = taps // 2
    length = values.shape[0]
    padded = jnp.pad(values, ((margin, margin), (0, 0)))
    grad_padded = jnp.pad(grad_out, ((margin, margin), (0, 0)))
    seg_padded = jnp.pad(segment, (margin, margin), constant_values=-1)
    value_grad = jnp.zeros_like(values)
    tap_rows = []
    for offset in range(taps):
        joined = (seg_padded[offset : offset + length] == segment).astype(jnp.float32)[:, None]
        tap_rows.append(jnp.sum(grad_out * joined * padded[offset : offset + length], axis=0))
        mirror = 2 * margin - offset
        back_joined = (seg_padded[mirror : mirror + length] == segment).astype(jnp.float32)[:, None]
        value_grad = (
            value_grad
            + grad_padded[mirror : mirror + length] * back_joined * kernel[offset][None, :]
        )
    return (value_grad, jnp.stack(tap_rows, axis=0))


def body(
    block_input,
    w_value,
    b_value,
    conv_kernel,
    w_out,
    b_out,
    gain_attn,
    shift_attn,
    w_up,
    b_up,
    w_down,
    b_down,
    gain_ffn,
    shift_ffn,
    query_codes,
    key_codes,
    key_live,
    seq_lengths,
    out_grad,
):
    length = block_input.shape[0]
    model_width = block_input.shape[1]
    head_dim = model_width // HEADS
    live_keys = key_live.astype(jnp.float32)[:, None]
    seq_ends = jnp.cumsum(seq_lengths[0], dtype=jnp.int32)
    positions = jnp.arange(length, dtype=jnp.int32)
    segment = jnp.sum(
        (seq_ends[None, :] <= positions[:, None]).astype(jnp.int32), axis=1, dtype=jnp.int32
    )
    query_heads = query_codes.reshape(length, HEADS, SETS).transpose(1, 0, 2)
    key_heads = key_codes.reshape(length, HEADS, SETS).transpose(1, 0, 2)
    joined = (segment[:, None] == segment[None, :]).astype(jnp.float32)
    bucket_ids = jnp.arange(BUCKETS, dtype=jnp.int32)

    def head_counts(pair):
        query_set, key_set = pair
        query_hot = (
            (query_set[:, :, None] == bucket_ids[None, None, :])
            .astype(jnp.bfloat16)
            .reshape(length, SETS * BUCKETS)
        )
        key_hot = (
            (key_set[:, :, None] == bucket_ids[None, None, :])
            .astype(jnp.bfloat16)
            .reshape(length, SETS * BUCKETS)
        )
        counts = dot_last(query_hot, key_hot)
        return (counts * joined / SETS).astype(jnp.bfloat16)

    collide = lax.map(head_counts, (query_heads, key_heads))
    kernel_f = conv_kernel.astype(jnp.float32)
    value_pre = jnp.dot(block_input, w_value, preferred_element_type=jnp.float32) + b_value.astype(
        jnp.float32
    )
    values = value_pre.astype(jnp.bfloat16)
    masked = values.astype(jnp.float32) * live_keys
    masked_low = masked.astype(jnp.bfloat16)
    mixed = jnp.einsum(
        "hij,jhd->ihd",
        collide,
        masked_low.reshape(length, HEADS, head_dim),
        preferred_element_type=jnp.float32,
    ).reshape(length, model_width)
    normed, norm_back = jax.vjp(partial(head_norm, head_count=HEADS, head_dim=head_dim), mixed)
    context = (normed + depth_conv(masked, kernel_f, segment)).astype(jnp.bfloat16)
    attended = jnp.dot(context, w_out, preferred_element_type=jnp.float32) + b_out.astype(
        jnp.float32
    )
    first, first_back = jax.vjp(
        layer_norm,
        block_input.astype(jnp.float32) + attended,
        gain_attn.astype(jnp.float32),
        shift_attn.astype(jnp.float32),
    )
    first_low = first.astype(jnp.bfloat16)
    gathered = lax.all_gather(first_low, "tensor", axis=0, tiled=True)
    upper = jnp.dot(gathered, w_up, preferred_element_type=jnp.float32) + b_up.astype(jnp.float32)
    active_f, gelu_back = jax.vjp(gelu_exact, upper)
    active = active_f.astype(jnp.bfloat16)
    branch = lax.psum_scatter(
        jnp.dot(active, w_down, preferred_element_type=jnp.float32).astype(jnp.bfloat16),
        "tensor",
        scatter_dimension=0,
        tiled=True,
    ).astype(jnp.float32) + b_down.astype(jnp.float32)
    block_output, second_back = jax.vjp(
        layer_norm, first + branch, gain_ffn.astype(jnp.float32), shift_ffn.astype(jnp.float32)
    )
    grad_second, grad_gain_ffn, grad_shift_ffn = second_back(out_grad.astype(jnp.float32))
    branch_grad = grad_second.astype(jnp.bfloat16)
    grad_b_down = jnp.sum(branch_grad.astype(jnp.float32), axis=0)
    grad_rows_all = lax.all_gather(branch_grad, "tensor", axis=0, tiled=True)
    active_grad = dot_last(grad_rows_all, w_down)
    grad_w_down = dot_first(active, grad_rows_all)
    upper_grad = gelu_back(active_grad)[0].astype(jnp.bfloat16)
    grad_w_up = dot_first(gathered, upper_grad)
    grad_b_up = jnp.sum(upper_grad.astype(jnp.float32), axis=0)
    first_grad_ffn = lax.psum_scatter(
        dot_last(upper_grad, w_up).astype(jnp.bfloat16), "tensor", scatter_dimension=0, tiled=True
    ).astype(jnp.float32)
    first_grad = grad_second + first_grad_ffn
    resid_grad, grad_gain_attn, grad_shift_attn = first_back(first_grad)
    attended_grad = resid_grad.astype(jnp.bfloat16)
    grad_b_out = jnp.sum(attended_grad.astype(jnp.float32), axis=0)
    grad_w_out = dot_first(context, attended_grad)
    context_grad = dot_last(attended_grad, w_out)
    mixed_grad = norm_back(context_grad)[0].astype(jnp.bfloat16)
    conv_value_grad, grad_kernel = conv_back(context_grad, masked, kernel_f, segment)
    masked_att = jnp.einsum(
        "hij,ihd->jhd",
        collide,
        mixed_grad.reshape(length, HEADS, head_dim),
        preferred_element_type=jnp.float32,
    ).reshape(length, model_width)
    value_grad = ((masked_att + conv_value_grad) * live_keys).astype(jnp.bfloat16)
    grad_b_value = jnp.sum(value_grad.astype(jnp.float32), axis=0)
    grad_w_value = dot_first(block_input, value_grad)
    input_grad = resid_grad + dot_last(value_grad, w_value)
    grad_w_up, grad_w_down, grad_b_up = (
        lax.psum(grad_w_up.astype(jnp.bfloat16), "dp").astype(jnp.float32),
        lax.psum(grad_w_down.astype(jnp.bfloat16), "dp").astype(jnp.float32),
        lax.psum(grad_b_up.astype(jnp.bfloat16), "dp").astype(jnp.float32),
    )
    (
        grad_w_value,
        grad_b_value,
        grad_kernel,
        grad_w_out,
        grad_b_out,
        grad_gain_attn,
        grad_shift_attn,
        grad_b_down,
        grad_gain_ffn,
        grad_shift_ffn,
    ) = lax.psum(
        (
            grad_w_value,
            grad_b_value,
            grad_kernel,
            grad_w_out,
            grad_b_out,
            grad_gain_attn,
            grad_shift_attn,
            grad_b_down,
            grad_gain_ffn,
            grad_shift_ffn,
        ),
        ("dp", "tensor"),
    )
    return (
        block_output.astype(jnp.bfloat16),
        input_grad,
        grad_w_value,
        grad_b_value,
        grad_kernel,
        grad_w_out,
        grad_b_out,
        grad_gain_attn,
        grad_shift_attn,
        grad_w_up,
        grad_b_up,
        grad_w_down,
        grad_b_down,
        grad_gain_ffn,
        grad_shift_ffn,
    )


def solution(mesh):
    return jax.shard_map(
        body,
        mesh=mesh,
        in_specs=(
            P(("dp", "tensor"), None),
            P(),
            P(),
            P(),
            P(),
            P(),
            P(),
            P(),
            P(None, "tensor"),
            P("tensor"),
            P("tensor", None),
            P(),
            P(),
            P(),
            P(("dp", "tensor"), None),
            P(("dp", "tensor"), None),
            P(("dp", "tensor")),
            P(("dp", "tensor"), None),
            P(("dp", "tensor"), None),
        ),
        out_specs=(
            P(("dp", "tensor"), None),
            P(("dp", "tensor"), None),
            P(),
            P(),
            P(),
            P(),
            P(),
            P(),
            P(),
            P(None, "tensor"),
            P("tensor"),
            P("tensor", None),
            P(),
            P(),
            P(),
        ),
        check_vma=False,
    )
```

profile of v0, /device:TPU:1, one launch (start us, length us, event | category | flops | bytes accessed | tf_op | source)
XLA Modules:
  0.0 701.4 jit_solution(10940862884612107198)
XLA Ops:
  17.3 43.1 %while.12 = (s32[]{:T(128)}, bf16[12,256,256]{2,1,0:T(8,128)(2,1)}, s32[12,256,32]{1,2,0:T(8,128)S(1)}, s32[12,256,32]{1,2,0:T(8,128)S(1)}, s32[256]{0:T(256)S(1)}, /*index=5*/s32[]{:T(128)}) while((s32[]{:T(128)}, bf16[12,256,256]{2,1,0:T(8,128)(2,1)}, s32[12,256,32]{1,2,0:T(8,128)S(1)}, s32[12,256,32]{1,2,0:T(8,128)S(1)}, ...), condition=%wide.region_3.4_spmd.clone.clone, body=%wide.region_2.3_spmd.clone.clone.sunk | while | flops 1078198272 | bytes 330313 | solution.py:125
  17.4 3.6 fusion.266
  21.0 3.6 fusion.266
  24.6 3.6 fusion.266
  28.1 3.6 fusion.266
  31.7 3.6 fusion.266
  35.3 3.6 fusion.266
  38.9 3.6 fusion.266
  42.5 3.6 fusion.266
  46.1 3.6 fusion.266
  49.7 3.6 fusion.266
  53.3 3.6 fusion.266
  56.8 3.6 fusion.266
  66.3 11.6 %add_convert_fusion.2 = bf16[256,768]{1,0:T(8,128)(2,1)S(1)} fusion(f32[256,768]{1,0:T(8,128)S(1)} %copy.51, f32[256,768]{1,0:T(8,128)S(1)} %get-tuple-element.368, f32[768]{0:T(1024)} %get-tuple-element.198, f32[256]{0:T(256)} %get-tuple-element.366, f32[768]{0:T(1024)} %get-tuple-element.199, f32[256]{0:T(256)} %get-tuple-element.365, ...), kind=kLoop, calls=%fused_computation.456 | loop fusion | flops 38338560 | bytes 2231296 | tf_op jit(solution)/shard_map/convert_element_type | solution.py:140
  83.6 11.4 %reduce-scatter.3.cloned.1.call-start = ((), (), s32[]{:S(2)}) async-start(), calls=%async_computation.3 | async-start | bytes 3538944 | tf_op jit(solution)/shard_map/reduce_scatter | solution.py:155
  96.2 53.2 %all-gather.3.cloned.1.call-done = bf16[2048,768]{1,0:T(8,128)(2,1)} async-done(((bf16[256,768]{1,0:T(8,128)(2,1)}), bf16[2048,768]{1,0:T(8,128)(2,1)}) %all-gather.3.cloned.1.call-update) | async-done | bytes 3145744 | tf_op jit(solution)/shard_map/all_gather | solution.py:151
  149.4 11.6 %multiply_convert_fusion = (bf16[2048,384]{1,0:T(8,128)(2,1)S(1)}, f32[2048,384]{1,0:T(8,128)}, f32[2048,384]{1,0:T(8,128)}) fusion(f32[384]{0:T(512)} %convert_element_type.529, bf16[2048,768]{1,0:T(8,128)(2,1)} %all-gather.3.cloned.1.call-done, bf16[768,384]{1,0:T(8,128)(2,1)} %param.29), kind=kOutput, calls=%fused_computation.148 | convolution fusion | flops 1259864064 | bytes 11601408 | tf_op jit(solution)/shard_map/dot_general | solution.py:152
  162.2 3.4 convolution_convert_fusion.1
  169.5 72.7 %reduce-scatter.3.cloned.1.call-done = bf16[256,768]{1,0:T(8,128)(2,1)} async-done(((bf16[2048,768]{1,0:T(8,128)(2,1)}), bf16[256,768]{1,0:T(8,128)(2,1)}) %reduce-scatter.3.cloned.1.call-update) | async-done | bytes 393232 | tf_op jit(solution)/shard_map/reduce_scatter | solution.py:155
  249.4 62.5 %all-gather.5.cloned.1.call-done = bf16[2048,768]{1,0:T(8,128)(2,1)} async-done(((bf16[256,768]{1,0:T(8,128)(2,1)}), bf16[2048,768]{1,0:T(8,128)(2,1)}) %all-gather.5.cloned.1.call-update) | async-done | bytes 3145744 | tf_op jit(solution)/shard_map/all_gather | solution.py:167
  311.9 7.3 %fusion.230 = (bf16[384]{0:T(512)(128)(2,1)}, bf16[2048,384]{1,0:T(8,128)(2,1)S(1)}) fusion(f32[2048,384]{1,0:T(8,128)} %get-tuple-element.299, f32[2048,384]{1,0:T(8,128)} %get-tuple-element.373, bf16[2048,768]{1,0:T(8,128)(2,1)} %all-gather.5.cloned.1.call-done, bf16[384,768]{1,0:T(8,128)(2,1)} %param.31), kind=kOutput, calls=%fused_computation.674 | convolution fusion | flops 1219755648 | bytes 11600640 | tf_op jit(solution)/shard_map/dot_general | solution.py:13
  320.4 3.5 convolution_convert_fusion
  324.0 4.8 convolution_convert_fusion.2
  331.5 69.1 %reduce-scatter.5.cloned.1.call-done = bf16[256,768]{1,0:T(8,128)(2,1)} async-done(((bf16[2048,768]{1,0:T(8,128)(2,1)}), bf16[256,768]{1,0:T(8,128)(2,1)}) %reduce-scatter.5.cloned.1.call-update) | async-done | bytes 393232 | tf_op jit(solution)/shard_map/reduce_scatter | solution.py:173
  451.9 5.8 stack.263
  457.7 11.7 %convert_reduce_fusion.3 = (f32[768]{0:T(1024)S(1)}, bf16[256,768]{1,0:T(8,128)(2,1)S(1)}) fusion(f32[256]{0:T(256)} %copy-done.110, f32[256,768]{1,0:T(8,128)S(1)} %copy.53, f32[768]{0:T(1024)} %get-tuple-element.198, f32[256]{0:T(256)} %get-tuple-element.303, f32[768]{0:T(1024)} %get-tuple-element.199, f32[256]{0:T(256)} %get-tuple-element.321, ...), kind=kLoop, calls=%fused_computation.446 | loop fusion | flops 38927616 | bytes 2235392 | tf_op jit(solution)/shard_map/reduce_sum | solution.py:191
  472.0 28.5 %psum.99 = bf16[384]{0:T(512)(128)(2,1)S(1)} all-reduce(bf16[384]{0:T(512)(128)(2,1)S(1)} %copy-done.120), channel_id=1, replica_groups=mesh['dp'=16,'tensor'=8] {'dp'}, use_global_device_ids=true, to_apply=%region_94.95 | all-reduce | flops 384 | bytes 1536 | tf_op jit(solution)/shard_map/psum | solution.py:197
  501.1 22.6 %all-reduce.11.cloned.1.call-done = (bf16[768,384]{1,0:T(8,128)(2,1)}, bf16[384,768]{1,0:T(8,128)(2,1)}) async-done(((bf16[768,384]{1,0:T(8,128)(2,1)}, bf16[384,768]{1,0:T(8,128)(2,1)}), (bf16[768,384]{1,0:T(8,128)(2,1)}, bf16[384,768]{1,0:T(8,128)(2,1)})) %all-reduce.11.cloned.1.call-update) | async-done | bytes 1179664 | tf_op jit(solution)/shard_map/psum | solution.py:195
  528.0 68.4 %all-reduce.3 = (f32[768]{0:T(1024)}, f32[768]{0:T(1024)}, f32[768]{0:T(1024)}, f32[768]{0:T(1024)}, f32[768]{0:T(1024)}, /*index=5*/f32[768]{0:T(1024)}, f32[768]{0:T(1024)}) all-reduce(f32[768]{0:T(1024)S(1)} %get-tuple-element.290, f32[768]{0:T(1024)S(1)} %copy-done.37, ...), channel_id=1, replica_groups=mesh['dp'=16,'tensor'=8] {'dp','tensor'}, use_global_device_ids=true, to_apply=%region_18.19 | all-reduce | flops 5376 | bytes 43008 | tf_op jit(solution)/shard_map/psum | solution.py:210
  597.9 89.3 %all-reduce.9.cloned.1.call-done = (f32[768,768]{0,1:T(8,128)}, f32[65,768]{1,0:T(8,128)}, f32[768,768]{1,0:T(8,128)}) async-done(((f32[768,768]{0,1:T(8,128)}, f32[65,768]{1,0:T(8,128)}, f32[768,768]{1,0:T(8,128)}), (f32[768,768]{0,1:T(8,128)}, f32[65,768]{1,0:T(8,128)}, f32[768,768]{1,0:T(8,128)})) %all-reduce.9.cloned.1.call-update) | async-done | bytes 4918288 | tf_op jit(solution)/shard_map/psum | solution.py:210
  687.1 3.1 copy.54
  690.9 3.2 copy.70
  (405 shorter events, 98.2 us)
Async XLA Ops:
  7.2 53.3 %copy-start = (bf16[768,768]{1,0:T(8,128)(2,1)S(1)}, bf16[768,768]{1,0:T(8,128)(2,1)}, u32[]{:S(2)}) copy-start(bf16[768,768]{1,0:T(8,128)(2,1)} %param.22) | copy-start | bytes 3538948
  7.2 142.2 %all-gather.3.cloned.1.call-start = ((), (), s32[]{:S(2)}) async-start(), calls=%async_computation.2 | async-start | bytes 3538944 | tf_op jit(solution)/shard_map/all_gather | solution.py:151
  17.3 43.1 %copy-start.119 = (s32[256]{0:T(256)S(1)}, s32[256]{0:T(256)}, u32[]{:S(2)}) copy-start(s32[256]{0:T(256)} %param.37) | copy-start | bytes 3076
  17.3 43.1 %copy-start.116 = (bf16[768]{0:T(1024)(128)(2,1)S(1)}, bf16[768]{0:T(1024)(128)(2,1)}, u32[]{:S(2)}) copy-start(bf16[768]{0:T(1024)(128)(2,1)} %param.23) | copy-start | bytes 4612
  17.3 43.1 %copy-start.6 = (bf16[256,768]{1,0:T(8,128)(2,1)S(1)}, bf16[256,768]{1,0:T(8,128)(2,1)}, u32[]{:S(2)}) copy-start(bf16[256,768]{1,0:T(8,128)(2,1)} %param.21) | copy-start | bytes 1179652
  83.6 158.7 %reduce-scatter.3.cloned.1.call-start = ((), (), s32[]{:S(2)}) async-start(), calls=%async_computation.3 | async-start | bytes 3538944 | tf_op jit(solution)/shard_map/reduce_scatter | solution.py:155
  165.6 146.3 %all-gather.5.cloned.1.call-start = ((), (), s32[]{:S(2)}) async-start(), calls=%async_computation.4 | async-start | bytes 3538944 | tf_op jit(solution)/shard_map/all_gather | solution.py:167
  249.3 151.3 %reduce-scatter.5.cloned.1.call-start = ((), (), s32[]{:S(2)}) async-start(), calls=%async_computation.5 | async-start | bytes 3538944 | tf_op jit(solution)/shard_map/reduce_scatter | solution.py:173
  323.9 199.8 %all-reduce.11.cloned.1.call-start = ((), (), s32[]{:S(2)}) async-start(), calls=%async_computation.7 | async-start | bytes 2359296 | tf_op jit(solution)/shard_map/psum | solution.py:195
  331.4 355.7 %all-reduce.9.cloned.1.call-start = ((), (), s32[]{:S(2)}) async-start(), calls=%async_computation.6 | async-start | bytes 9879552 | tf_op jit(solution)/shard_map/psum | solution.py:210
  429.1 21.1 %copy-start.50 = (f32[768]{0:T(1024)S(1)}, f32[768]{0:T(1024)}, u32[]{:S(2)}) copy-start(f32[768]{0:T(1024)} %get-tuple-element.158) | copy-start | bytes 9220
  429.1 21.1 %copy-start.49 = (f32[768]{0:T(1024)S(1)}, f32[768]{0:T(1024)}, u32[]{:S(2)}) copy-start(f32[768]{0:T(1024)} %get-tuple-element.157) | copy-start | bytes 9220
  429.1 21.2 %copy-start.48 = (f32[768]{0:T(1024)S(1)}, f32[768]{0:T(1024)}, u32[]{:S(2)}) copy-start(f32[768]{0:T(1024)} %get-tuple-element.156) | copy-start | bytes 9220
  429.1 21.2 %copy-start.47 = (f32[768]{0:T(1024)S(1)}, f32[768]{0:T(1024)}, u32[]{:S(2)}) copy-start(f32[768]{0:T(1024)} %get-tuple-element.155) | copy-start | bytes 9220
  429.1 21.2 %copy-start.46 = (f32[768]{0:T(1024)S(1)}, f32[768]{0:T(1024)}, u32[]{:S(2)}) copy-start(f32[768]{0:T(1024)} %get-tuple-element.190) | copy-start | bytes 9220
  429.1 21.2 %copy-start.45 = (f32[768]{0:T(1024)S(1)}, f32[768]{0:T(1024)}, u32[]{:S(2)}) copy-start(f32[768]{0:T(1024)} %get-tuple-element.189) | copy-start | bytes 9220
  429.2 21.2 %copy-start.44 = (f32[768]{0:T(1024)S(1)}, f32[768]{0:T(1024)}, u32[]{:S(2)}) copy-start(f32[768]{0:T(1024)} %get-tuple-element.188) | copy-start | bytes 9220
  429.2 21.2 %copy-start.43 = (f32[768]{0:T(1024)S(1)}, f32[768]{0:T(1024)}, u32[]{:S(2)}) copy-start(f32[768]{0:T(1024)} %get-tuple-element.187) | copy-start | bytes 9220
  429.2 21.2 %copy-start.42 = (f32[768]{0:T(1024)S(1)}, f32[768]{0:T(1024)}, u32[]{:S(2)}) copy-start(f32[768]{0:T(1024)} %get-tuple-element.186) | copy-start | bytes 9220
  429.2 21.2 %copy-start.41 = (f32[768]{0:T(1024)S(1)}, f32[768]{0:T(1024)}, u32[]{:S(2)}) copy-start(f32[768]{0:T(1024)} %get-tuple-element.185) | copy-start | bytes 9220
  429.2 21.3 %copy-start.40 = (f32[768]{0:T(1024)S(1)}, f32[768]{0:T(1024)}, u32[]{:S(2)}) copy-start(f32[768]{0:T(1024)} %get-tuple-element.184) | copy-start | bytes 9220
  429.2 21.3 %copy-start.39 = (f32[768]{0:T(1024)S(1)}, f32[768]{0:T(1024)}, u32[]{:S(2)}) copy-start(f32[768]{0:T(1024)} %get-tuple-element.183) | copy-start | bytes 9220
  429.2 21.3 %copy-start.38 = (f32[768]{0:T(1024)S(1)}, f32[768]{0:T(1024)}, u32[]{:S(2)}) copy-start(f32[768]{0:T(1024)} %get-tuple-element.182) | copy-start | bytes 9220
  430.6 38.8 %copy-start.7 = (bf16[256,768]{1,0:T(8,128)(2,1)S(1)}, bf16[256,768]{1,0:T(8,128)(2,1)}, u32[]{:S(2)}) copy-start(bf16[256,768]{1,0:T(8,128)(2,1)} %param.21) | copy-start | bytes 1179652
  471.3 56.7 %copy-start.32 = (f32[768]{0:T(1024)S(1)}, f32[768]{0:T(1024)}, u32[]{:S(2)}) copy-start(f32[768]{0:T(1024)} %get-tuple-element.193) | copy-start | bytes 9220
  471.3 56.7 %copy-start.33 = (f32[768]{0:T(1024)S(1)}, f32[768]{0:T(1024)}, u32[]{:S(2)}) copy-start(f32[768]{0:T(1024)} %get-tuple-element.196) | copy-start | bytes 9220
  471.3 56.7 %copy-start.34 = (f32[768]{0:T(1024)S(1)}, f32[768]{0:T(1024)}, u32[]{:S(2)}) copy-start(f32[768]{0:T(1024)} %get-tuple-element.286) | copy-start | bytes 9220
  471.3 56.7 %copy-start.35 = (f32[768]{0:T(1024)S(1)}, f32[768]{0:T(1024)}, u32[]{:S(2)}) copy-start(f32[768]{0:T(1024)} %get-tuple-element.126) | copy-start | bytes 9220
  471.3 56.7 %copy-start.36 = (f32[768]{0:T(1024)S(1)}, f32[768]{0:T(1024)}, u32[]{:S(2)}) copy-start(f32[768]{0:T(1024)} %get-tuple-element.195) | copy-start | bytes 9220
  471.4 56.7 %copy-start.37 = (f32[768]{0:T(1024)S(1)}, f32[768]{0:T(1024)}, u32[]{:S(2)}) copy-start(f32[768]{0:T(1024)} %get-tuple-element.288) | copy-start | bytes 9220
  471.4 125.1 %copy-start.3 = (f32[256,768]{1,0:T(8,128)S(1)}, f32[256,768]{1,0:T(8,128)}, u32[]{:S(2)}) copy-start(f32[256,768]{1,0:T(8,128)} %copy-done.2) | copy-start | bytes 2359300
  471.4 125.1 %copy-start.115 = (f32[256]{0:T(256)S(1)}, f32[256]{0:T(256)}, u32[]{:S(2)}) copy-start(f32[256]{0:T(256)} %copy-done.114) | copy-start | bytes 3076
  (98 other events, 990.9 us)
Sparse Core Ops, SparseCore 0:
  83.7 65.6 all-gather.2
  165.7 76.4 reduce-scatter.2
  249.5 62.4 all-gather.4
  324.0 76.5 reduce-scatter.4
  403.6 120.0 all-reduce.10
  529.7 157.4 all-reduce.8
where the time goes:
time: 710 us; the launch traced here: 701 us
  waiting for transfers between devices  369 us (52%)
  blocking collectives  97 us (14%)
  matrix products  88.4 us (12%)
  other arithmetic  70.4 us (10%)
  local copies, waits for them, and re-layouts  48.2 us (7%)
  between operations  16.4 us (2%)
  starting transfers between devices  11.6 us (2%)
    psum x1, waiting for transfers between devices, body(): lax.psum((grad_w_value, grad_b_value, grad_kernel, grad_w_out, grad_b_out...  89.3 us
    reduce_scatter x1, waiting for transfers between devices, body(): lax.psum_scatter(jnp.dot(active, w_down, preferred_element_type=jnp.float...  72.7 us
    reduce_scatter x1, waiting for transfers between devices, body(): lax.psum_scatter(dot_last(upper_grad, w_up).astype(jnp.bfloat16), 'tensor...  69.1 us
    psum x1, blocking collectives, body(): lax.psum((grad_w_value, grad_b_value, grad_kernel, grad_w_out, grad_b_out...  68.4 us
    all_gather x1, waiting for transfers between devices, body(): grad_rows_all = lax.all_gather(branch_grad, 'tensor', axis=0, tiled=True)  62.5 us
    dot_general x16, matrix products, dot_last(): lax.dot_general(former, latter, (((1,), (1,)), ((), ())), preferred_eleme...  56.4 us
    all_gather x1, waiting for transfers between devices, body(): gathered = lax.all_gather(first_low, 'tensor', axis=0, tiled=True)  53.2 us
    psum x1, blocking collectives, body(): lax.psum(grad_b_up.astype(jnp.bfloat16), 'dp').astype(jnp.float32)  28.5 us
  transfers between devices with their start and end apart: 6, of which 6 were waited for; matrix products, arithmetic and copies ran while one was open for 12% of the time, Pallas kernels for 0%

commit v1 on v0

--- a/solution.py
+++ b/solution.py
@@ -208,19 +208,22 @@
         grad_gain_ffn,
         grad_shift_ffn,
     ) = lax.psum(
-        (
-            grad_w_value,
-            grad_b_value,
-            grad_kernel,
-            grad_w_out,
-            grad_b_out,
-            grad_gain_attn,
-            grad_shift_attn,
-            grad_b_down,
-            grad_gain_ffn,
-            grad_shift_ffn,
+        lax.psum(
+            (
+                grad_w_value,
+                grad_b_value,
+                grad_kernel,
+                grad_w_out,
+                grad_b_out,
+                grad_gain_attn,
+                grad_shift_attn,
+                grad_b_down,
+                grad_gain_ffn,
+                grad_shift_ffn,
+            ),
+            "tensor",
         ),
-        ("dp", "tensor"),
+        "dp",
     )
     return (
         block_output.astype(jnp.bfloat16),

time: 710 us -> 898 us (1.26)
  waiting for transfers between devices: 369 us -> 524 us
  local copies, waits for them, and re-layouts: 48.2 us -> 70.4 us
  blocking collectives: 97 us -> 118 us
  starting transfers between devices: 11.6 us -> 1.14 us
    psum x1, waiting for transfers between devices: 22.6 us -> 93.8 us  [body(): lax.psum(grad_w_up.astype(jnp.bfloat16), 'dp').astype(jnp.float32)]
    psum x0 -> x1, blocking collectives: none -> 56.4 us  [body(): lax.psum(lax.psum((grad_w_value, grad_b_value, grad_kernel, grad_w_out, g...]
    psum x0 -> x1, waiting for transfers between devices: none -> 39.1 us  [body(): lax.psum(lax.psum((grad_w_value, grad_b_value, grad_kernel, grad_w_out, g...]
    psum x1, blocking collectives: 68.4 us -> 34.6 us  [body(): lax.psum((grad_w_value, grad_b_value, grad_kernel, grad_w_out, grad_b_out...]
    psum x1, waiting for transfers between devices: 89.3 us -> 115 us  [body(): lax.psum((grad_w_value, grad_b_value, grad_kernel, grad_w_out, grad_b_out...]
    another operation x66, local copies, waits for them, and re-layouts: 25 us -> 48 us  [conv_back(): return (value_grad, jnp.stack(tap_rows, axis=0))]
    all_gather x1, waiting for transfers between devices: 53.2 us -> 64 us  [body(): gathered = lax.all_gather(first_low, 'tensor', axis=0, tiled=True)]
    reduce_scatter x1, starting transfers between devices: 11.4 us -> 0.51 us  [body(): lax.psum_scatter(jnp.dot(active, w_down, preferred_element_type=jnp.float...]
  transfers between devices with their start and end apart: 6 -> 7, of which waited for: 6 -> 7; matrix products, arithmetic and copies ran while one was open for 12% -> 2% of each run, Pallas kernels for 0% -> 0%
where the time goes in v1:
time: 898 us; the launch traced here: 888 us
  waiting for transfers between devices  524 us (58%)
  blocking collectives  118 us (13%)
  matrix products  88.3 us (10%)
  other arithmetic  70.7 us (8%)
  local copies, waits for them, and re-layouts  70.4 us (8%)
  between operations  15.4 us (2%)
    psum x1, waiting for transfers between devices, body(): lax.psum((grad_w_value, grad_b_value, grad_kernel, grad_w_out, grad_b_out...  115 us
    psum x1, waiting for transfers between devices, body(): lax.psum(grad_w_up.astype(jnp.bfloat16), 'dp').astype(jnp.float32)  93.8 us
    reduce_scatter x1, waiting for transfers between devices, body(): lax.psum_scatter(dot_last(upper_grad, w_up).astype(jnp.bfloat16), 'tensor...  76.5 us
    reduce_scatter x1, waiting for transfers between devices, body(): lax.psum_scatter(jnp.dot(active, w_down, preferred_element_type=jnp.float...  72.7 us
    all_gather x1, waiting for transfers between devices, body(): gathered = lax.all_gather(first_low, 'tensor', axis=0, tiled=True)  64 us
    all_gather x1, waiting for transfers between devices, body(): grad_rows_all = lax.all_gather(branch_grad, 'tensor', axis=0, tiled=True)  62.5 us
    psum x1, blocking collectives, body(): lax.psum(lax.psum((grad_w_value, grad_b_value, grad_kernel, grad_w_out, g...  56.4 us
    dot_general x16, matrix products, dot_last(): lax.dot_general(former, latter, (((1,), (1,)), ((), ())), preferred_eleme...  56.4 us
  transfers between devices with their start and end apart: 7, of which 7 were waited for; matrix products, arithmetic and copies ran while one was open for 2% of the time, Pallas kernels for 0%

profile of v1, /device:TPU:1, one launch (start us, length us, event | category | flops | bytes accessed | tf_op | source)
XLA Modules:
  0.0 888.1 jit_solution(9586789266774734349)
XLA Ops:
  17.3 43.1 %while.12 = (s32[]{:T(128)}, bf16[12,256,256]{2,1,0:T(8,128)(2,1)}, s32[12,256,32]{1,2,0:T(8,128)S(1)}, s32[12,256,32]{1,2,0:T(8,128)S(1)}, s32[256]{0:T(256)S(1)}, /*index=5*/s32[]{:T(128)}) while((s32[]{:T(128)}, bf16[12,256,256]{2,1,0:T(8,128)(2,1)}, s32[12,256,32]{1,2,0:T(8,128)S(1)}, s32[12,256,32]{1,2,0:T(8,128)S(1)}, ...), condition=%wide.region_3.4_spmd.clone.clone, body=%wide.region_2.3_spmd.clone.clone.sunk | while | flops 1078198272 | bytes 330313 | solution.py:125
  17.4 3.6 fusion.266
  21.0 3.6 fusion.266
  24.5 3.6 fusion.266
  28.1 3.6 fusion.266
  31.7 3.6 fusion.266
  35.3 3.6 fusion.266
  38.9 3.6 fusion.266
  42.5 3.6 fusion.266
  46.1 3.6 fusion.266
  49.7 3.6 fusion.266
  53.2 3.6 fusion.266
  56.8 3.6 fusion.266
  66.3 11.6 %add_convert_fusion.2 = bf16[256,768]{1,0:T(8,128)(2,1)S(1)} fusion(f32[256,768]{1,0:T(8,128)S(1)} %copy.51, f32[256,768]{1,0:T(8,128)S(1)} %get-tuple-element.378, f32[768]{0:T(1024)} %get-tuple-element.198, f32[256]{0:T(256)} %get-tuple-element.376, f32[768]{0:T(1024)} %get-tuple-element.199, f32[256]{0:T(256)} %get-tuple-element.375, ...), kind=kLoop, calls=%fused_computation.456 | loop fusion | flops 38338560 | bytes 2231296 | tf_op jit(solution)/shard_map/convert_element_type | solution.py:140
  85.4 64.0 %all-gather.3.cloned.1.call-done = bf16[2048,768]{1,0:T(8,128)(2,1)} async-done(((bf16[256,768]{1,0:T(8,128)(2,1)}), bf16[2048,768]{1,0:T(8,128)(2,1)}) %all-gather.3.cloned.1.call-update) | async-done | bytes 3145744 | tf_op jit(solution)/shard_map/all_gather | solution.py:151
  149.4 11.5 %multiply_convert_fusion = (bf16[2048,384]{1,0:T(8,128)(2,1)S(1)}, f32[2048,384]{1,0:T(8,128)}, f32[2048,384]{1,0:T(8,128)}) fusion(f32[384]{0:T(512)} %convert_element_type.529, bf16[2048,768]{1,0:T(8,128)(2,1)} %all-gather.3.cloned.1.call-done, bf16[768,384]{1,0:T(8,128)(2,1)} %param.29), kind=kOutput, calls=%fused_computation.148 | convolution fusion | flops 1259864064 | bytes 11601408 | tf_op jit(solution)/shard_map/dot_general | solution.py:152
  162.1 3.5 convolution_convert_fusion.1
  169.5 72.7 %reduce-scatter.3.cloned.1.call-done = bf16[256,768]{1,0:T(8,128)(2,1)} async-done(((bf16[2048,768]{1,0:T(8,128)(2,1)}), bf16[256,768]{1,0:T(8,128)(2,1)}) %reduce-scatter.3.cloned.1.call-update) | async-done | bytes 393232 | tf_op jit(solution)/shard_map/reduce_scatter | solution.py:155
  249.4 62.5 %all-gather.5.cloned.1.call-done = bf16[2048,768]{1,0:T(8,128)(2,1)} async-done(((bf16[256,768]{1,0:T(8,128)(2,1)}), bf16[2048,768]{1,0:T(8,128)(2,1)}) %all-gather.5.cloned.1.call-update) | async-done | bytes 3145744 | tf_op jit(solution)/shard_map/all_gather | solution.py:167
  311.9 7.3 fusion.230
  320.4 3.5 convolution_convert_fusion
  324.2 76.5 %reduce-scatter.5.cloned.1.call-done = bf16[256,768]{1,0:T(8,128)(2,1)} async-done(((bf16[2048,768]{1,0:T(8,128)(2,1)}), bf16[256,768]{1,0:T(8,128)(2,1)}) %reduce-scatter.5.cloned.1.call-update) | async-done | bytes 393232 | tf_op jit(solution)/shard_map/reduce_scatter | solution.py:173
  431.6 12.1 %convert_reduce_fusion.3 = (f32[768]{0:T(1024)S(1)}, bf16[256,768]{1,0:T(8,128)(2,1)S(1)}) fusion(f32[256]{0:T(256)} %copy-done.76, f32[256,768]{1,0:T(8,128)S(1)} %copy.53, f32[768]{0:T(1024)} %get-tuple-element.198, f32[256]{0:T(256)} %get-tuple-element.313, f32[768]{0:T(1024)} %get-tuple-element.199, f32[256]{0:T(256)} %get-tuple-element.331, ...), kind=kLoop, calls=%fused_computation.446 | loop fusion | flops 38927616 | bytes 2235392 | tf_op jit(solution)/shard_map/reduce_sum | solution.py:191
  487.9 5.8 stack.263
  494.0 4.7 convolution_convert_fusion.2
  501.4 114.9 %all-reduce.14.cloned.1.call-done = (f32[768,768]{0,1:T(8,128)}, f32[65,768]{1,0:T(8,128)}, f32[768,768]{1,0:T(8,128)}) async-done(((f32[768,768]{0,1:T(8,128)}, f32[65,768]{1,0:T(8,128)}, f32[768,768]{1,0:T(8,128)}), (f32[768,768]{0,1:T(8,128)}, f32[65,768]{1,0:T(8,128)}, f32[768,768]{1,0:T(8,128)})) %all-reduce.14.cloned.1.call-update) | async-done | bytes 4918288 | tf_op jit(solution)/shard_map/psum | solution.py:211
  616.4 27.3 %psum.176 = bf16[384]{0:T(512)(128)(2,1)S(1)} all-reduce(bf16[384]{0:T(512)(128)(2,1)S(1)} %copy-done.86), channel_id=1, replica_groups=mesh['dp'=16,'tensor'=8] {'dp'}, use_global_device_ids=true, to_apply=%region_101.102 | all-reduce | flops 384 | bytes 1536 | tf_op jit(solution)/shard_map/psum | solution.py:197
  644.4 93.8 %all-reduce.16.cloned.1.call-done = (bf16[768,384]{1,0:T(8,128)(2,1)}, bf16[384,768]{1,0:T(8,128)(2,1)}) async-done(((bf16[768,384]{1,0:T(8,128)(2,1)}, bf16[384,768]{1,0:T(8,128)(2,1)}), (bf16[768,384]{1,0:T(8,128)(2,1)}, bf16[384,768]{1,0:T(8,128)(2,1)})) %all-reduce.16.cloned.1.call-update) | async-done | bytes 1179664 | tf_op jit(solution)/shard_map/psum | solution.py:195
  742.5 34.6 %all-reduce.5 = (f32[768]{0:T(1024)S(1)}, f32[768]{0:T(1024)S(1)}, f32[768]{0:T(1024)S(1)}, f32[768]{0:T(1024)S(1)}, f32[768]{0:T(1024)S(1)}, /*index=5*/f32[768]{0:T(1024)S(1)}, f32[768]{0:T(1024)S(1)}) all-reduce(f32[768]{0:T(1024)S(1)} %get-tuple-element.300, ...), channel_id=1, replica_groups=mesh['dp'=16,'tensor'=8] {'tensor'}, use_global_device_ids=true, to_apply=%region_19.20 | all-reduce | flops 5376 | bytes 43008 | tf_op jit(solution)/shard_map/psum | solution.py:211
  777.1 56.4 %all-reduce.3 = (f32[768]{0:T(1024)}, f32[768]{0:T(1024)}, f32[768]{0:T(1024)}, f32[768]{0:T(1024)}, f32[768]{0:T(1024)}, /*index=5*/f32[768]{0:T(1024)}, f32[768]{0:T(1024)}) all-reduce(f32[768]{0:T(1024)S(1)} %get-tuple-element.282, f32[768]{0:T(1024)S(1)} %get-tuple-element.283, ...), channel_id=1, replica_groups=mesh['dp'=16,'tensor'=8] {'dp'}, use_global_device_ids=true, to_apply=%region_20.21 | all-reduce | flops 5376 | bytes 43008 | tf_op jit(solution)/shard_map/psum | solution.py:210
  834.9 39.1 %all-reduce.12.cloned.1.call-done = (f32[768,768]{0,1:T(8,128)}, f32[65,768]{1,0:T(8,128)}, f32[768,768]{1,0:T(8,128)}) async-done(((f32[768,768]{0,1:T(8,128)}, f32[65,768]{1,0:T(8,128)}, f32[768,768]{1,0:T(8,128)}), (f32[768,768]{0,1:T(8,128)}, f32[65,768]{1,0:T(8,128)}, f32[768,768]{1,0:T(8,128)})) %all-reduce.12.cloned.1.call-update) | async-done | bytes 4918288 | tf_op jit(solution)/shard_map/psum | solution.py:210
  877.8 3.2 copy.73
  (341 shorter events, 124.3 us)
Async XLA Ops:
  7.2 53.3 %copy-start = (bf16[768,768]{1,0:T(8,128)(2,1)S(1)}, bf16[768,768]{1,0:T(8,128)(2,1)}, u32[]{:S(2)}) copy-start(bf16[768,768]{1,0:T(8,128)(2,1)} %param.22) | copy-start | bytes 3538948
  7.2 142.2 %all-gather.3.cloned.1.call-start = ((), (), s32[]{:S(2)}) async-start(), calls=%async_computation.2 | async-start | bytes 3538944 | tf_op jit(solution)/shard_map/all_gather | solution.py:151
  17.3 43.1 %copy-start.85 = (s32[256]{0:T(256)S(1)}, s32[256]{0:T(256)}, u32[]{:S(2)}) copy-start(s32[256]{0:T(256)} %param.37) | copy-start | bytes 3076
  17.3 43.1 %copy-start.82 = (bf16[768]{0:T(1024)(128)(2,1)S(1)}, bf16[768]{0:T(1024)(128)(2,1)}, u32[]{:S(2)}) copy-start(bf16[768]{0:T(1024)(128)(2,1)} %param.23) | copy-start | bytes 4612
  17.3 43.1 %copy-start.6 = (bf16[256,768]{1,0:T(8,128)(2,1)S(1)}, bf16[256,768]{1,0:T(8,128)(2,1)}, u32[]{:S(2)}) copy-start(bf16[256,768]{1,0:T(8,128)(2,1)} %param.21) | copy-start | bytes 1179652
  65.6 15.9 %copy-start.83 = (bf16[768]{0:T(1024)(128)(2,1)S(1)}, bf16[768]{0:T(1024)(128)(2,1)}, u32[]{:S(2)}) copy-start(bf16[768]{0:T(1024)(128)(2,1)} %param.27) | copy-start | bytes 4612
  65.6 15.9 %copy-start.84 = (bf16[768]{0:T(1024)(128)(2,1)S(1)}, bf16[768]{0:T(1024)(128)(2,1)}, u32[]{:S(2)}) copy-start(bf16[768]{0:T(1024)(128)(2,1)} %param.28) | copy-start | bytes 4612
  83.6 158.7 %reduce-scatter.3.cloned.1.call-start = ((), (), s32[]{:S(2)}) async-start(), calls=%async_computation.3 | async-start | bytes 3538944 | tf_op jit(solution)/shard_map/reduce_scatter | solution.py:155
  149.4 12.7 %copy-start.87 = (bf16[384,768]{1,0:T(8,128)(2,1)S(1)}, bf16[384,768]{1,0:T(8,128)(2,1)}, u32[]{:S(2)}) copy-start(bf16[384,768]{1,0:T(8,128)(2,1)} %param.31) | copy-start | bytes 1769476
  165.6 146.3 %all-gather.5.cloned.1.call-start = ((), (), s32[]{:S(2)}) async-start(), calls=%async_computation.4 | async-start | bytes 3538944 | tf_op jit(solution)/shard_map/all_gather | solution.py:167
  249.4 151.3 %reduce-scatter.5.cloned.1.call-start = ((), (), s32[]{:S(2)}) async-start(), calls=%async_computation.5 | async-start | bytes 3538944 | tf_op jit(solution)/shard_map/reduce_scatter | solution.py:173
  323.9 292.4 %all-reduce.14.cloned.1.call-start = ((), (), s32[]{:S(2)}) async-start(), calls=%async_computation.7 | async-start | bytes 9879552 | tf_op jit(solution)/shard_map/psum | solution.py:211
  413.7 10.4 %copy-start.27 = (f32[256]{0:T(256)S(1)}, f32[256]{0:T(256)}, u32[]{:S(2)}) copy-start(f32[256]{0:T(256)} %get-tuple-element.343) | copy-start | bytes 3076
  413.7 10.5 %copy-start.28 = (f32[256]{0:T(256)S(1)}, f32[256]{0:T(256)}, u32[]{:S(2)}) copy-start(f32[256]{0:T(256)} %get-tuple-element.344) | copy-start | bytes 3076
  413.7 10.5 %copy-start.29 = (f32[256]{0:T(256)S(1)}, f32[256]{0:T(256)}, u32[]{:S(2)}) copy-start(f32[256]{0:T(256)} %get-tuple-element.345) | copy-start | bytes 3076
  413.7 10.5 %copy-start.30 = (f32[256]{0:T(256)S(1)}, f32[256]{0:T(256)}, u32[]{:S(2)}) copy-start(f32[256]{0:T(256)} %get-tuple-element.346) | copy-start | bytes 3076
  413.7 10.5 %copy-start.31 = (f32[256]{0:T(256)S(1)}, f32[256]{0:T(256)}, u32[]{:S(2)}) copy-start(f32[256]{0:T(256)} %get-tuple-element.347) | copy-start | bytes 3076
  430.1 54.4 %copy-start.40 = (f32[768]{0:T(1024)S(1)}, f32[768]{0:T(1024)}, u32[]{:S(2)}) copy-start(f32[768]{0:T(1024)} %get-tuple-element.184) | copy-start | bytes 9220
  430.1 54.4 %copy-start.39 = (f32[768]{0:T(1024)S(1)}, f32[768]{0:T(1024)}, u32[]{:S(2)}) copy-start(f32[768]{0:T(1024)} %get-tuple-element.183) | copy-start | bytes 9220
  430.1 54.5 %copy-start.38 = (f32[768]{0:T(1024)S(1)}, f32[768]{0:T(1024)}, u32[]{:S(2)}) copy-start(f32[768]{0:T(1024)} %get-tuple-element.182) | copy-start | bytes 9220
  430.1 55.8 %copy-start.7 = (bf16[256,768]{1,0:T(8,128)(2,1)S(1)}, bf16[256,768]{1,0:T(8,128)(2,1)}, u32[]{:S(2)}) copy-start(bf16[256,768]{1,0:T(8,128)(2,1)} %param.21) | copy-start | bytes 1179652
  493.7 244.4 %all-reduce.16.cloned.1.call-start = ((), (), s32[]{:S(2)}) async-start(), calls=%async_computation.8 | async-start | bytes 2359296 | tf_op jit(solution)/shard_map/psum | solution.py:195
  501.4 115.1 %copy-start.86 = (bf16[384]{0:T(512)(128)(2,1)S(1)}, bf16[384]{0:T(512)(128)(2,1)}, u32[]{:S(2)}) copy-start(bf16[384]{0:T(512)(128)(2,1)} %get-tuple-element.294) | copy-start | bytes 2308
  501.4 372.6 %all-reduce.12.cloned.1.call-start = ((), (), s32[]{:S(2)}) async-start(), calls=%async_computation.6 | async-start | bytes 9879552 | tf_op jit(solution)/shard_map/psum | solution.py:210
  616.4 126.1 %copy-start.32 = (f32[768]{0:T(1024)S(1)}, f32[768]{0:T(1024)}, u32[]{:S(2)}) copy-start(f32[768]{0:T(1024)} %get-tuple-element.193) | copy-start | bytes 9220
  616.4 126.1 %copy-start.33 = (f32[768]{0:T(1024)S(1)}, f32[768]{0:T(1024)}, u32[]{:S(2)}) copy-start(f32[768]{0:T(1024)} %get-tuple-element.196) | copy-start | bytes 9220
  616.4 126.1 %copy-start.34 = (f32[768]{0:T(1024)S(1)}, f32[768]{0:T(1024)}, u32[]{:S(2)}) copy-start(f32[768]{0:T(1024)} %get-tuple-element.296) | copy-start | bytes 9220
  616.4 126.1 %copy-start.35 = (f32[768]{0:T(1024)S(1)}, f32[768]{0:T(1024)}, u32[]{:S(2)}) copy-start(f32[768]{0:T(1024)} %get-tuple-element.126) | copy-start | bytes 9220
  616.4 126.1 %copy-start.36 = (f32[768]{0:T(1024)S(1)}, f32[768]{0:T(1024)}, u32[]{:S(2)}) copy-start(f32[768]{0:T(1024)} %get-tuple-element.195) | copy-start | bytes 9220
  616.4 126.1 %copy-start.37 = (f32[768]{0:T(1024)S(1)}, f32[768]{0:T(1024)}, u32[]{:S(2)}) copy-start(f32[768]{0:T(1024)} %get-tuple-element.298) | copy-start | bytes 9220
  616.4 217.1 %copy-start.3 = (f32[256,768]{1,0:T(8,128)S(1)}, f32[256,768]{1,0:T(8,128)}, u32[]{:S(2)}) copy-start(f32[256,768]{1,0:T(8,128)} %copy-done.2) | copy-start | bytes 2359300
  616.4 217.1 %copy-start.81 = (f32[256]{0:T(256)S(1)}, f32[256]{0:T(256)}, u32[]{:S(2)}) copy-start(f32[256]{0:T(256)} %copy-done.80) | copy-start | bytes 3076
  (65 other events, 386.1 us)
Sparse Core Ops, SparseCore 0:
  83.7 65.6 all-gather.2
  165.8 76.4 reduce-scatter.2
  249.5 62.4 all-gather.4
  324.1 76.5 reduce-scatter.4
  493.8 122.4 all-reduce.13
  619.9 118.1 all-reduce.15
  740.9 133.0 all-reduce.11
